TPU v7x, 256 devices: a whole 4x4x8 slice. The times are simulated.
256 devices in a mesh: lon: 32 (over z, y_lo, core), lat: 8 (over x, y_hi).
Axes of the slice: x: 4, y: 4 (y_hi: 2, y_lo: 2; y = y_hi * 2 + y_lo), z: 8, core: 2. Of those that a mesh axis runs over, the one named last changes fastest.
Arguments:
- embeddings: bfloat16 [512, 2048, 128], P('lat', 'lon'), may hold values from -400 to 400
- query_owner: int32 [2, 64], replicated, may hold values from 0 to 255
- query_row: int32 [2, 64], replicated, may hold values from 0 to 59
- query_col: int32 [2, 64], replicated, may hold values from 0 to 59
Outputs:
- scores: float32 [512, 2048, 128], P('lat', 'lon')
Inputs may be any that keep to these rules, and one draw needn't show every extreme that they name: `query_row`: the exemplar lies inside its owner's tile. `query_col`: the exemplar lies inside its owner's tile.
All inputs are finite; a program needn't handle non-finite values.
Results may differ from a plain program's by a relative error of at most 0.0029.
Values may be sent and summed in bfloat16 or wider, within the bound.
A program may use at most 128 MiB of HBM per device.

v0:
```python
import jax
import jax.numpy as jnp
from jax import lax
from jax.sharding import PartitionSpec as P


def extended_2(x, sides, width):
    for axis, dim in sides:
        count, length = (lax.axis_size(axis), x.shape[dim])
        up = [(i, (i + 1) % count) for i in range(count)]
        down = [(j, i) for i, j in up]
        last = lax.slice_in_dim(x, length - width, length, axis=dim)
        first = lax.slice_in_dim(x, 0, width, axis=dim)
        before = lax.ppermute(last, axis, up)
        after = lax.ppermute(first, axis, down)
        x = jnp.concatenate([before, x, after], axis=dim)
    return x


def body(embeddings, query_owner, query_row, query_col):
    rows, cols, chans = embeddings.shape
    band = lax.axis_index("lat")
    strip = lax.axis_index("lon")
    here = band * lax.axis_size("lon") + strip
    owner = query_owner.reshape(-1)
    row_first = query_row.reshape(-1)
    col_first = query_col.reshape(-1)

    def take(row_one, col_one):
        zero = jnp.zeros((), jnp.int32)
        return lax.dynamic_slice(embeddings, (row_one, col_one, zero), (5, 5, chans))

    patches = jax.vmap(take, out_axes=3)(row_first, col_first).astype(jnp.float32)
    count = patches.shape[3]
    table = jnp.where((owner == here)[None, None, None, :], patches, 0.0)
    whole = lax.psum(table, ("lon", "lat"))
    mean_sq = jnp.mean(whole * whole, axis=(0, 1, 2))
    queries = (whole * lax.rsqrt(mean_sq + 1e-05)).astype(jnp.bfloat16)
    extended = extended_2(embeddings, (("lat", 0), ("lon", 1)), 2)
    row_index = jnp.arange(rows + 4, dtype=jnp.int32)[:, None, None]
    cut_top = (band == 0) & (row_index < 2)
    cut_bottom = (band == lax.axis_size("lat") - 1) & (row_index >= rows + 2)
    extended = jnp.where(cut_top | cut_bottom, jnp.zeros((), jnp.bfloat16), extended)
    total = jnp.zeros((rows * cols, count), jnp.float32)
    for shift_y in range(5):
        for shift_x in range(5):
            slab = extended[shift_y : shift_y + rows, shift_x : shift_x + cols, :].reshape(
                rows * cols, chans
            )
            total = total + jnp.dot(
                slab, queries[shift_y, shift_x], preferred_element_type=jnp.float32
            )
    squares = jnp.sum(jnp.square(extended.astype(jnp.float32)), axis=2)
    box_sum = jnp.zeros((rows, cols), jnp.float32)
    for shift_y in range(5):
        for shift_x in range(5):
            box_sum = box_sum + squares[shift_y : shift_y + rows, shift_x : shift_x + cols]
    energy = box_sum / (25 * chans)
    return total.reshape(rows, cols, count) * lax.rsqrt(25 * chans * (energy + 1e-05))[:, :, None]


def solution(mesh):
    placed = (P("lat", "lon", None), P(), P(), P())
    return jax.shard_map(
        body, mesh=mesh, in_specs=placed, out_specs=P("lat", "lon", None), check_vma=False
    )
```

profile of v0, /device:TPU:1, one launch (start us, length us, event | category | flops | bytes accessed | tf_op | source)
XLA Modules:
  0.0 668.3 jit_solution(10743078012196713790)
XLA Ops:
  7.3 5.9 collective-permute-start.1
  15.6 350.3 %while.1 = (s32[]{:T(128)}, bf16[64,64,128]{2,1,0:T(8,128)(2,1)}, s32[128,3]{0,1:T(4,128)S(1)}, bf16[128,5,5,128]{3,2,1,0:T(8,128)(2,1)S(1)}, s32[]{:T(128)}) while((s32[]{:T(128)}, bf16[64,64,128]{2,1,0:T(8,128)(2,1)}, s32[128,3]{0,1:T(4,128)S(1)}, bf16[128,5,5,128]{3,2,1,0:T(8,128)(2,1)S(1)}, s32[]{:T(128)}) %tuple.46), condition=%wide.while_cond, body=%wide.while_body.sunk | while | flops 2 | bytes 16765 | solution.py:31
  16.3 2.1 bitcast_dynamic-update-slice_fusion.2
  19.0 2.1 bitcast_dynamic-update-slice_fusion.2
  27.2 2.1 bitcast_dynamic-update-slice_fusion.2
  49.1 2.1 bitcast_dynamic-update-slice_fusion.2
  51.8 2.1 bitcast_dynamic-update-slice_fusion.2
  54.6 2.1 bitcast_dynamic-update-slice_fusion.2
  57.3 2.1 bitcast_dynamic-update-slice_fusion.2
  60.0 2.1 bitcast_dynamic-update-slice_fusion.2
  62.8 2.1 bitcast_dynamic-update-slice_fusion.2
  65.5 2.1 bitcast_dynamic-update-slice_fusion.2
  71.0 2.1 bitcast_dynamic-update-slice_fusion.2
  76.4 2.1 bitcast_dynamic-update-slice_fusion.2
  79.2 2.1 bitcast_dynamic-update-slice_fusion.2
  87.4 2.1 bitcast_dynamic-update-slice_fusion.2
  92.8 2.1 bitcast_dynamic-update-slice_fusion.2
  95.6 2.1 bitcast_dynamic-update-slice_fusion.2
  98.3 2.1 bitcast_dynamic-update-slice_fusion.2
  101.0 2.1 bitcast_dynamic-update-slice_fusion.2
  103.8 2.1 bitcast_dynamic-update-slice_fusion.2
  106.5 2.1 bitcast_dynamic-update-slice_fusion.2
  109.3 2.1 bitcast_dynamic-update-slice_fusion.2
  112.0 2.1 bitcast_dynamic-update-slice_fusion.2
  114.7 2.1 bitcast_dynamic-update-slice_fusion.2
  117.5 2.1 bitcast_dynamic-update-slice_fusion.2
  120.2 2.1 bitcast_dynamic-update-slice_fusion.2
  142.1 2.1 bitcast_dynamic-update-slice_fusion.2
  144.9 2.1 bitcast_dynamic-update-slice_fusion.2
  147.6 2.1 bitcast_dynamic-update-slice_fusion.2
  150.3 2.1 bitcast_dynamic-update-slice_fusion.2
  153.1 2.1 bitcast_dynamic-update-slice_fusion.2
  155.8 2.1 bitcast_dynamic-update-slice_fusion.2
  158.6 2.1 bitcast_dynamic-update-slice_fusion.2
  161.3 2.1 bitcast_dynamic-update-slice_fusion.2
  164.0 2.1 bitcast_dynamic-update-slice_fusion.2
  166.8 2.1 bitcast_dynamic-update-slice_fusion.2
  169.5 2.1 bitcast_dynamic-update-slice_fusion.2
  175.0 2.1 bitcast_dynamic-update-slice_fusion.2
  177.7 2.1 bitcast_dynamic-update-slice_fusion.2
  185.9 2.1 bitcast_dynamic-update-slice_fusion.2
  191.4 2.1 bitcast_dynamic-update-slice_fusion.2
  196.9 2.1 bitcast_dynamic-update-slice_fusion.2
  199.6 2.1 bitcast_dynamic-update-slice_fusion.2
  202.3 2.1 bitcast_dynamic-update-slice_fusion.2
  205.1 2.1 bitcast_dynamic-update-slice_fusion.2
  207.8 2.1 bitcast_dynamic-update-slice_fusion.2
  210.6 2.1 bitcast_dynamic-update-slice_fusion.2
  216.0 2.1 bitcast_dynamic-update-slice_fusion.2
  218.7 2.1 bitcast_dynamic-update-slice_fusion.2
  221.5 2.1 bitcast_dynamic-update-slice_fusion.2
  224.2 2.1 bitcast_dynamic-update-slice_fusion.2
  227.0 2.1 bitcast_dynamic-update-slice_fusion.2
  229.7 2.1 bitcast_dynamic-update-slice_fusion.2
  232.4 2.1 bitcast_dynamic-update-slice_fusion.2
  235.2 2.1 bitcast_dynamic-update-slice_fusion.2
  237.9 2.1 bitcast_dynamic-update-slice_fusion.2
  259.9 2.1 bitcast_dynamic-update-slice_fusion.2
  309.1 2.1 bitcast_dynamic-update-slice_fusion.2
  341.9 2.1 bitcast_dynamic-update-slice_fusion.2
  371.5 2.3 collective-permute-done.3
  375.4 3.4 fusion.7
  378.8 8.0 %fusion.6 = (bf16[64,64,128]{2,1,0:T(8,128)(2,1)S(1)}, bf16[64,64,128]{2,1,0:T(8,128)(2,1)S(1)}, bf16[64,64,128]{2,1,0:T(8,128)(2,1)S(1)}, bf16[64,64,128]{2,1,0...) fusion(bf16[68,68,128]{2,1,0:T(8,128)(2,1)S(1)} %get-tuple-elem, ...), kind=kLoop, calls=%fused_computation.96 | loop fusion | bytes 39845888 | tf_op jit(solution)/shard_map/slice | solution.py:47
  386.9 243.0 %all-reduce.2.cloned.1.call-done = f32[5,5,128,128]{3,2,1,0:T(8,128)} async-done(((f32[5,5,128,128]{3,2,1,0:T(8,128)}), f32[5,5,128,128]{3,2,1,0:T(8,128)}) %all-reduce.2.cloned.1.call-update) | async-done | bytes 1638416 | tf_op jit(solution)/shard_map/psum | solution.py:36
  (429 shorter events, 270.9 us)
Async XLA Ops:
  6.5 623.3 %all-reduce.2.cloned.1.call-start = ((), (), s32[]{:S(2)}) async-start(), calls=%async_computation | async-start | bytes 3276800 | tf_op jit(solution)/shard_map/psum | solution.py:36
  7.3 361.7 %collective-permute-start.1 = (bf16[2,64,128]{2,1,0:T(8,128)(2,1)S(1)}, bf16[2,64,128]{2,1,0:T(8,128)(2,1)S(1)}, u32[]{:S(2)}, u32[]{:S(2)}) collective-permute-start(bf16[2,64,128]{2,1,0:T(8,128)(2,1)S(1)} %get-tuple-element.52), channel_id=1, source_target_pairs={{1,0},{2,1},{3,2},{4,3},{5,4},{6,5},{7,6},{0,7},{9,8},{10,9},{11,1... | collective-permute-start | bytes 98312 | tf_op jit(solution)/shard_map/ppermute | solution.py:15
  13.3 355.5 %collective-permute-start = (bf16[2,64,128]{2,1,0:T(8,128)(2,1)S(1)}, bf16[2,64,128]{2,1,0:T(8,128)(2,1)S(1)}, u32[]{:S(2)}, u32[]{:S(2)}) collective-permute-start(bf16[2,64,128]{2,1,0:T(8,128)(2,1)S(1)} %get-tuple-element.53), channel_id=1, source_target_pairs={{0,1},{1,2},{2,3},{3,4},{4,5},{5,6},{6,7},{7,0},{8,9},{9,10},{10,1... | collective-permute-start | bytes 98312 | tf_op jit(solution)/shard_map/ppermute | solution.py:14
  367.4 1.5 copy-start.23
  369.1 2.4 collective-permute-start.2
  370.4 3.4 collective-permute-start.3
  629.9 2.0 copy-start
  629.9 2.3 copy-start.22
  632.1 1.2 copy-start.21
  633.4 1.2 copy-start.20
  634.6 1.2 copy-start.19
  635.8 1.2 copy-start.18
  637.0 1.2 copy-start.17
  638.3 1.2 copy-start.16
  639.5 1.2 copy-start.15
  640.7 1.2 copy-start.14
  641.9 1.2 copy-start.13
  643.2 1.2 copy-start.12
  644.4 1.2 copy-start.11
  645.6 1.2 copy-start.10
  646.8 1.2 copy-start.9
  648.1 1.2 copy-start.8
  649.3 1.2 copy-start.7
  650.5 1.2 copy-start.6
  651.7 1.2 copy-start.5
  653.0 1.2 copy-start.4
  654.2 1.2 copy-start.3
  655.4 1.2 copy-start.2
  656.6 1.2 copy-start.1
Sparse Core Ops, SparseCore 0:
  368.9 260.9 all-reduce.1
where the time goes:
time: 681 us; the launch traced here: 668 us
  local copies, waits for them, and re-layouts  381 us (56%)
  waiting for transfers between devices  246 us (36%)
  between operations  13.7 us (2%)
  matrix products  10.3 us (2%)
  other arithmetic  7.83 us (1%)
  starting transfers between devices  7.26 us (1%)
    gather x384, local copies, waits for them, and re-layouts  348 us
    psum x1, waiting for transfers between devices, body(): whole = lax.psum(table, ('lon', 'lat'))  243 us
    unnamed x50, local copies, waits for them, and re-layouts  17.1 us
  transfers between devices with their start and end apart: 5, of which 3 were waited for; matrix products, arithmetic and copies ran while one was open for 55% of the time, Pallas kernels for 0%

commit v1 on v0

v1 whole, which is shorter than its diff:
```python
import jax
import jax.numpy as jnp
from jax import lax
from jax.experimental import pallas as pl
from jax.experimental.pallas import tpu as pltpu
from jax.sharding import PartitionSpec as P

F32 = jnp.float32
BF16 = jnp.bfloat16
SLOTS = 26
EPS = 1e-05


def gather_kernel(own_ref, row_ref, col_ref, emb_ref, tab_ref, edge_ref, flat, tabf):
    here = lax.axis_index("lat") * lax.axis_size("lon") + lax.axis_index("lon")
    rows, cols, chans = emb_ref.shape
    panels, per_panel = own_ref.shape
    count = panels * per_panel

    @pl.loop(0, rows)
    def _(i):
        flat[pl.ds(pl.multiple_of(i * cols, cols), cols), :] = emb_ref[i].astype(F32)

    @pl.loop(0, SLOTS)
    def _(s):
        tabf[pl.ds(pl.multiple_of(s * count, count), count), :] = jnp.zeros((count, chans), F32)

    for side, first in ((0, 0), (1, cols - 2)):
        for c in range(2):
            edge_ref[side, c] = flat[pl.ds(first + c, rows, stride=cols), :].astype(BF16)

    for p in range(panels):

        @pl.loop(0, per_panel)
        def _(q):
            @pl.when(own_ref[p, q] == here)
            def _():
                base = row_ref[p, q] * cols + col_ref[p, q]
                for dy in range(5):
                    for dx in range(5):
                        tabf[pl.ds((dy * 5 + dx) * count + p * per_panel + q, 1), :] = flat[
                            pl.ds(base + dy * cols + dx, 1), :
                        ]

    @pl.loop(0, SLOTS)
    def _(s):
        tab_ref[s] = tabf[pl.ds(pl.multiple_of(s * count, count), count), :].astype(BF16)


def gather_table(owner, row, col, emb):
    rows, cols, chans = emb.shape
    count = owner.size
    smem = pl.BlockSpec(memory_space=pltpu.SMEM)
    vmem = pl.BlockSpec(memory_space=pltpu.VMEM)
    return pl.pallas_call(
        gather_kernel,
        out_shape=(
            jax.ShapeDtypeStruct((SLOTS, count, chans), BF16),
            jax.ShapeDtypeStruct((2, 2, rows, chans), BF16),
        ),
        in_specs=[smem, smem, smem, vmem],
        out_specs=(vmem, vmem),
        scratch_shapes=[
            pltpu.VMEM((rows * cols, chans), F32),
            pltpu.VMEM((SLOTS * count, chans), F32),
        ],
        compiler_params=pltpu.CompilerParams(vmem_limit_bytes=16 << 20),
        name="gather_table",
    )(owner, row, col, emb)


def score_kernel(q_ref, emb_ref, rowh_ref, colh_ref, corn_ref, out_ref, ext, shifted, qn, inv, band_sum):
    rows, cols, chans = emb_ref.shape
    count = q_ref.shape[1]
    band = lax.axis_index("lat")
    top = (band != 0).astype(F32)
    bottom = (band != lax.axis_size("lat") - 1).astype(F32)

    @pl.loop(0, rows)
    def _(i):
        ext[i + 2, 8 : 8 + cols, :] = emb_ref[i].astype(F32)

    for r in range(2):
        ext[r, 8 : 8 + cols, :] = rowh_ref[0, r].astype(F32) * top
        ext[rows + 2 + r, 8 : 8 + cols, :] = rowh_ref[1, r].astype(F32) * bottom
    for c in range(2):
        ext[2 : 2 + rows, 6 + c : 7 + c, :] = colh_ref[0, c].astype(F32)[:, None, :]
        ext[2 : 2 + rows, 8 + cols + c : 9 + cols + c, :] = colh_ref[1, c].astype(F32)[:, None, :]
        for side, at in ((0, 6 + c), (1, 8 + cols + c)):
            above = corn_ref[side, c].astype(F32) * top
            below = corn_ref[2 + side, c].astype(F32) * bottom
            for r in range(2):
                ext[r, at : at + 1, :] = above[6 + r : 7 + r]
                ext[rows + 2 + r, at : at + 1, :] = below[r : r + 1]

    @pl.loop(0, rows + 4)
    def _(i):
        for dx in range(5):
            shifted[i, :, dx * chans : (dx + 1) * chans] = ext[i, 6 + dx : 6 + dx + cols, :].astype(BF16)

    @pl.loop(0, rows)
    def _(i):
        column = jnp.zeros((cols + 16, chans), F32)
        for dy in range(5):
            column = column + jnp.square(ext[i + dy])
        band_sum[...] = column
        box = jnp.zeros((cols, chans), F32)
        for dx in range(5):
            box = box + band_sum[6 + dx : 6 + dx + cols, :]
        energy = jnp.sum(box, axis=1, keepdims=True) / (25 * chans)
        inv[i] = jnp.broadcast_to(lax.rsqrt(25 * chans * (energy + EPS)), (cols, chans))

    total = jnp.zeros((count, chans), F32)
    for s in range(25):
        total = total + jnp.square(q_ref[s].astype(F32))
    scale = lax.rsqrt(jnp.sum(total, axis=1, keepdims=True) / (25 * chans) + EPS)
    for s in range(25):
        qn[:, s * chans : (s + 1) * chans] = (q_ref[s].astype(F32) * scale).astype(BF16)

    block = 8

    @pl.loop(0, rows // block)
    def _(b):
        acc = jnp.zeros((block * cols, count), F32)
        for dy in range(5):
            lhs = shifted[pl.ds(b * block + dy, block)].reshape(block * cols, 5 * chans)
            rhs = qn[:, dy * 5 * chans : (dy + 1) * 5 * chans]
            acc = acc + lax.dot_general(lhs, rhs, (((1,), (1,)), ((), ())), preferred_element_type=F32)
        out_ref[pl.ds(b * block, block)] = acc.reshape(block, cols, count) * inv[pl.ds(b * block, block)]


def score(q, emb, rowh, colh, corn):
    rows, cols, chans = emb.shape
    count = q.shape[1]
    vmem = pl.BlockSpec(memory_space=pltpu.VMEM)
    return pl.pallas_call(
        score_kernel,
        out_shape=jax.ShapeDtypeStruct((rows, cols, count), F32),
        in_specs=[vmem] * 5,
        out_specs=vmem,
        scratch_shapes=[
            pltpu.VMEM((rows + 4, cols + 16, chans), F32),
            pltpu.VMEM((rows + 4, cols, 5 * chans), BF16),
            pltpu.VMEM((count, 25 * chans), BF16),
            pltpu.VMEM((rows, cols, chans), F32),
            pltpu.VMEM((cols + 16, chans), F32),
        ],
        compiler_params=pltpu.CompilerParams(vmem_limit_bytes=48 << 20),
        name="score",
    )(q, emb, rowh, colh, corn)


def body(embeddings, query_owner, query_row, query_col):
    table, edge = gather_table(query_owner, query_row, query_col, embeddings)
    queries = lax.psum(table, ("lon", "lat"))
    lon = lax.axis_size("lon")
    lat = lax.axis_size("lat")
    up = [(i, (i + 1) % lat) for i in range(lat)]
    down = [(j, i) for i, j in up]
    right = [(i, (i + 1) % lon) for i in range(lon)]
    left = [(j, i) for i, j in right]
    rowh = jnp.stack([lax.ppermute(embeddings[-2:], "lat", up), lax.ppermute(embeddings[:2], "lat", down)])
    colh = jnp.stack([lax.ppermute(edge[1], "lon", right), lax.ppermute(edge[0], "lon", left)])
    above = lax.ppermute(colh[:, :, -8:], "lat", up)
    below = lax.ppermute(colh[:, :, :8], "lat", down)
    return score(queries, embeddings, rowh, colh, jnp.concatenate([above, below]))


def solution(mesh):
    placed = (P("lat", "lon", None), P(), P(), P())
    return jax.shard_map(
        body, mesh=mesh, in_specs=placed, out_specs=P("lat", "lon", None), check_vma=False
    )
```

time: 681 us -> 304 us (0.45); the launches traced: 668 us -> 304 us
  local copies, waits for them, and re-layouts: 381 us -> 4.43 us
  Pallas kernels: 0 us -> 22.9 us
  matrix products: 10.3 us -> 0 us
  other arithmetic: 7.83 us -> 0.03 us
    gather x385 -> x0, local copies, waits for them, and re-layouts: 350 us -> none
    pallas_call x0 -> x2, Pallas kernels: none -> 22.9 us  [the longest x1 18.6 us: score(): pl.pallas_call(score_kernel, out_shape=jax.ShapeDtypeStruct((rows, cols,...]
    unnamed x50 -> x12, local copies, waits for them, and re-layouts: 17.1 us -> 4.42 us
    slice x4 -> x1, local copies, waits for them, and re-layouts: 12.3 us -> 0.01 us  [body(): embeddings[-2:]]
    dot_general x25 -> x0, matrix products: 10.3 us -> none  [body(): jnp.dot(slab, queries[shift_y, shift_x], preferred_element_type=jnp.float32)]
  transfers between devices with their start and end apart: 5 -> 7, of which waited for: 3 -> 2; matrix products, arithmetic and copies ran while one was open for 55% -> 0% of each run, Pallas kernels for 0% -> 0%
where the time goes in v1:
time: 304 us
  waiting for transfers between devices  249 us (82%)
  Pallas kernels  22.9 us (8%)
  starting transfers between devices  13.6 us (4%)
  between operations  13.4 us (4%)
  local copies, waits for them, and re-layouts  4.43 us (1%)
    psum x1, waiting for transfers between devices, body(): queries = lax.psum(table, ('lon', 'lat'))  248 us
    pallas_call x1, Pallas kernels, score(): pl.pallas_call(score_kernel, out_shape=jax.ShapeDtypeStruct((rows, cols,...  18.6 us
  transfers between devices with their start and end apart: 7, of which 2 were waited for; matrix products, arithmetic and copies ran while one was open for 0% of the time, Pallas kernels for 0%

profile of v1, /device:TPU:1, one launch (start us, length us, event | category | flops | bytes accessed | tf_op | source)
XLA Modules:
  0.0 303.5 jit_solution(17691908439745221425)
XLA Ops:
  6.5 0.0 all-reduce.2.cloned.1.call-start
  6.5 0.0 copy-start
  6.5 1.2 copy-done
  7.8 0.0 copy-start.3
  7.8 0.7 copy-done.3
  8.4 0.0 copy-start.4
  8.4 0.7 copy-done.4
  9.1 0.0 copy-start.5
  9.1 0.7 copy-done.5
  9.8 0.0 copy-start.1
  9.8 4.3 %gather_table.1 = (bf16[26,128,128]{2,1,0:T(8,128)(2,1)}, bf16[2,2,64,128]{3,2,1,0:T(8,128)(2,1)S(1)}) custom-call(s32[2,64]{1,0:T(2,128)S(1)} %copy-done.3, s32[2,64]{1,0:T(2,128)S(1)} %copy-done.4, s32[2,64]{1,0:T(2,128)S(1)} %copy-done.5, bf16[64,64,128]{2,1,0:T(8,128)(2,1)S(1)} %copy-done), custom_call_target="tpu_custom_call" | custom-call | tf_op jit(solution)/shard_map/gather_table/pallas_call | solution.py:55
  14.1 2.7 collective-permute-start.2
  16.8 0.6 collective-permute-start.3
  17.4 2.0 collective-permute-start
  19.5 3.0 %collective-permute-start.1 = (bf16[2,64,128]{2,1,0:T(8,128)(2,1)S(1)}, bf16[2,64,128]{2,1,0:T(8,128)(2,1)S(1)}, u32[]{:S(2)}, u32[]{:S(2)}) collective-permute-start(bf16[2,64,128]{2,1,0:T(8,128)(2,1)S(1)} %get-tuple-element.10), channel_id=1, source_target_pairs={{1,0},{2,1},{3,2},{4,3},{5,4},{6,5},{7,6},{0,7},{9,8},{10,9},{11,1... | collective-permute-start | bytes 98312 | tf_op jit(solution)/shard_map/ppermute | solution.py:162
  22.5 0.0 all-reduce.2.cloned.1.call-update
  22.6 0.0 collective-permute-done.2
  22.6 0.0 collective-permute-done.3
  22.6 0.2 collective-permute-start.4
  22.8 4.9 %collective-permute-start.5 = (bf16[2,2,8,128]{3,2,1,0:T(8,128)(2,1)S(1)}, bf16[2,2,8,128]{3,2,1,0:T(8,128)(2,1)S(1)}, u32[]{:S(2)}, u32[]{:S(2)}) collective-permute-start(bf16[2,2,8,128]{3,2,1,0:T(8,128)(2,1)S(1)} %get-tuple-element.12), channel_id=1, source_target_pairs={{1,0},{2,1},{3,2},{4,3},{5,4},{6,5},{7,6},{0,7},{9,8},{10,9},{11,1... | collective-permute-start | bytes 24584 | tf_op jit(solution)/shard_map/ppermute | solution.py:165
  27.8 0.0 collective-permute-done
  27.8 0.0 collective-permute-done.1
  27.8 1.4 collective-permute-done.4
  29.2 0.0 collective-permute-done.5
  29.2 247.8 %all-reduce.2.cloned.1.call-done.q_ref = bf16[26,128,128]{2,1,0:T(8,128)(2,1)} async-done(((bf16[26,128,128]{2,1,0:T(8,128)(2,1)}), bf16[26,128,128]{2,1,0:T(8,128)(2,1)}) %all-reduce.2.cloned.1.call-update) | async-done | bytes 851984 | tf_op jit(solution)/shard_map/psum | solution.py:155
  276.9 0.0 copy-done.1
  277.0 0.0 copy-start.2
  277.0 1.2 copy-done.2
  278.1 18.6 %score.1 = f32[64,64,128]{2,1,0:T(8,128)} custom-call(bf16[26,128,128]{2,1,0:T(8,128)(2,1)S(1)} %copy-done.2, bf16[64,64,128]{2,1,0:T(8,128)(2,1)S(1)} %copy-done.1, bf16[2,2,64,128]{3,2,1,0:T(8,128)(2,1)S(1)} %pad_maximum_fusion.1.rowh_ref, bf16[2,2,64,128]{3,2,1,0:T(8,128)(2,1)S(1)} %pad_maximum_fusion.colh_ref, ...), custom_call_target="tpu_custom_call" | custom-call | tf_op jit(solution)/shard_map/score/pallas_call | solution.py:136
  (6 shorter events, 0.0 us)
Async XLA Ops:
  6.5 270.4 %all-reduce.2.cloned.1.call-start = ((), (), s32[]{:S(2)}) async-start(), calls=%async_computation | async-start | bytes 1703936 | tf_op jit(solution)/shard_map/psum | solution.py:155
  6.5 1.2 copy-start
  7.8 0.7 copy-start.3
  8.4 0.7 copy-start.4
  9.1 0.7 copy-start.5
  9.8 267.1 %copy-start.1 = (bf16[64,64,128]{2,1,0:T(8,128)(2,1)S(1)}, bf16[64,64,128]{2,1,0:T(8,128)(2,1)}, u32[]{:S(2)}) copy-start(bf16[64,64,128]{2,1,0:T(8,128)(2,1)} %emb_ref.3) | copy-start | bytes 3145732
  14.1 8.4 %collective-permute-start.2 = (bf16[2,64,128]{2,1,0:T(8,128)(2,1)S(1)}, bf16[2,64,128]{2,1,0:T(8,128)(2,1)S(1)}, u32[]{:S(2)}, u32[]{:S(2)}) collective-permute-start(bf16[2,64,128]{2,1,0:T(8,128)(2,1)S(1)} %get-tuple-element.13), channel_id=1, source_target_pairs={{0,8},{8,16},{16,24},{24,32},{32,40},{40,48},{48,56},{56,64},{64,7... | collective-permute-start | bytes 98312 | tf_op jit(solution)/shard_map/ppermute | solution.py:163
  16.8 5.8 %collective-permute-start.3 = (bf16[2,64,128]{2,1,0:T(8,128)(2,1)S(1)}, bf16[2,64,128]{2,1,0:T(8,128)(2,1)S(1)}, u32[]{:S(2)}, u32[]{:S(2)}) collective-permute-start(bf16[2,64,128]{2,1,0:T(8,128)(2,1)S(1)} %get-tuple-element.14), channel_id=1, source_target_pairs={{8,0},{16,8},{24,16},{32,24},{40,32},{48,40},{56,48},{64,56},{72,6... | collective-permute-start | bytes 98312 | tf_op jit(solution)/shard_map/ppermute | solution.py:163
  17.4 10.3 %collective-permute-start = (bf16[2,64,128]{2,1,0:T(8,128)(2,1)S(1)}, bf16[2,64,128]{2,1,0:T(8,128)(2,1)S(1)}, u32[]{:S(2)}, u32[]{:S(2)}) collective-permute-start(bf16[2,64,128]{2,1,0:T(8,128)(2,1)S(1)} %get-tuple-element.9), channel_id=1, source_target_pairs={{0,1},{1,2},{2,3},{3,4},{4,5},{5,6},{6,7},{7,0},{8,9},{9,10},{10,1... | collective-permute-start | bytes 98312 | tf_op jit(solution)/shard_map/ppermute | solution.py:162
  19.5 8.3 %collective-permute-start.1 = (bf16[2,64,128]{2,1,0:T(8,128)(2,1)S(1)}, bf16[2,64,128]{2,1,0:T(8,128)(2,1)S(1)}, u32[]{:S(2)}, u32[]{:S(2)}) collective-permute-start(bf16[2,64,128]{2,1,0:T(8,128)(2,1)S(1)} %get-tuple-element.10), channel_id=1, source_target_pairs={{1,0},{2,1},{3,2},{4,3},{5,4},{6,5},{7,6},{0,7},{9,8},{10,9},{11,1... | collective-permute-start | bytes 98312 | tf_op jit(solution)/shard_map/ppermute | solution.py:162
  22.6 6.6 %collective-permute-start.4 = (bf16[2,2,8,128]{3,2,1,0:T(8,128)(2,1)S(1)}, bf16[2,2,8,128]{3,2,1,0:T(8,128)(2,1)S(1)}, u32[]{:S(2)}, u32[]{:S(2)}) collective-permute-start(bf16[2,2,8,128]{3,2,1,0:T(8,128)(2,1)S(1)} %get-tuple-element.11), channel_id=1, source_target_pairs={{0,1},{1,2},{2,3},{3,4},{4,5},{5,6},{6,7},{7,0},{8,9},{9,10},{10,1... | collective-permute-start | bytes 24584 | tf_op jit(solution)/shard_map/ppermute | solution.py:164
  22.8 6.3 %collective-permute-start.5 = (bf16[2,2,8,128]{3,2,1,0:T(8,128)(2,1)S(1)}, bf16[2,2,8,128]{3,2,1,0:T(8,128)(2,1)S(1)}, u32[]{:S(2)}, u32[]{:S(2)}) collective-permute-start(bf16[2,2,8,128]{3,2,1,0:T(8,128)(2,1)S(1)} %get-tuple-element.12), channel_id=1, source_target_pairs={{1,0},{2,1},{3,2},{4,3},{5,4},{6,5},{7,6},{0,7},{9,8},{10,9},{11,1... | collective-permute-start | bytes 24584 | tf_op jit(solution)/shard_map/ppermute | solution.py:165
  277.0 1.2 copy-start.2
Sparse Core Ops, SparseCore 0:
  22.7 254.2 all-reduce.1
